TPU v7x, 32 devices: a whole 2x2x4 slice. The times are simulated.
32 devices in a mesh: ctx: 4 (over z), node: 4 (over y, core), local: 2 (over x).
Axes of the slice: x: 2, y: 2, z: 4, core: 2. Of those that a mesh axis runs over, the one named last changes fastest.
Arguments:
- tokens: bfloat16 [1024, 3584], P(('node', 'local'), 'ctx'), may hold values from -6 to 6
- expert_ids: int32 [1024, 4], P(('node', 'local')), may hold values from 0 to 7, as said below
- route_scores: float32 [1024, 4], P(('node', 'local')), may hold values from 0.05 to 1
- w_gate: bfloat16 [8, 3584, 2048], P(('node', 'local'), None, 'ctx'), may hold values from -0.09375 to 0.09375
- w_up: bfloat16 [8, 3584, 2048], P(('node', 'local'), None, 'ctx'), may hold values from -0.09375 to 0.09375
- w_down: bfloat16 [8, 2048, 3584], P(('node', 'local'), None, 'ctx'), may hold values from -0.125 to 0.125
- shared_gate: bfloat16 [3584, 2048], P(None, 'ctx'), may hold values from -0.09375 to 0.09375
- shared_up: bfloat16 [3584, 2048], P(None, 'ctx'), may hold values from -0.09375 to 0.09375
- shared_down: bfloat16 [2048, 3584], P(None, 'ctx'), may hold values from -0.125 to 0.125
Outputs:
- mixed: bfloat16 [1024, 3584], P(('node', 'local'), 'ctx')
Inputs may be any that keep to these rules, and one draw needn't show every extreme that they name: `expert_ids`: each row names 4 different experts: two in each of two different node groups, where expert e lies in group e // 2. In each aligned block of 128 rows (the rows of one index of node+local) no group is named by more than 80 rows and no expert more than 80 times; one group, the same in every block, is named by exactly 80 rows in every block, and one of its experts, the same in every block, exactly 80 times.
All inputs are finite; a program needn't handle non-finite values.
Results may differ from a plain program's by a relative error of at most 0.0064.
Values may be sent and summed in bfloat16 or wider, within the bound.
A program may use at most 64 MiB of HBM per device.

v0:
```python
import jax
import jax.numpy as jnp
from jax import lax
from jax.experimental import pallas as pl
from jax.experimental.pallas import tpu as pltpu
from jax.sharding import PartitionSpec as P

route_scale = 2.5
MESH = pl.DeviceIdType.MESH
VMEM_BYTES = 64000 * 1024


def matmul(left_side, right_side):
    return jnp.dot(left_side, right_side, preferred_element_type=jnp.float32)


def exchange(
    tokens, expert_ids, route_scores, w_gate, w_up, w_down, shared_gate, shared_up, shared_down
):
    tok_count = tokens.shape[0]
    feat_local = tokens.shape[1]
    top_count = expert_ids.shape[1]
    group_count = lax.axis_size("node")
    member_count = lax.axis_size("local")
    expert_count = group_count * member_count
    group_cap = (10 * tok_count + 4 * group_count - 1) // (4 * group_count)
    capacity = (2 * group_cap + member_count - 1) // member_count
    slot_total = expert_count * capacity
    gate_local = w_gate[0]
    up_local = w_up[0]
    down_local = w_down[0]
    out_width = down_local.shape[1]
    scaled = route_scale * route_scores / jnp.sum(route_scores, axis=1, keepdims=True)
    gate_weights = lax.optimization_barrier(scaled.astype(jnp.bfloat16)).astype(jnp.float32)
    group_range = jnp.arange(group_count, dtype=jnp.int32)
    group_onehot = (expert_ids // member_count)[:, :, None] == group_range[None, None, :]
    flat_ids = expert_ids.reshape(-1)
    pair_count = flat_ids.shape[0]
    onehot = (flat_ids[:, None] == jnp.arange(expert_count, dtype=jnp.int32)[None, :]).astype(
        jnp.int32
    )
    earlier = jnp.cumsum(onehot, axis=0) - onehot
    ranking = jnp.sum(earlier * onehot, axis=1)
    pair_slot = flat_ids * capacity + ranking
    pair_token = jnp.arange(pair_count, dtype=jnp.int32) // top_count
    matches = pair_slot[None, :] == jnp.arange(slot_total, dtype=jnp.int32)[:, None]
    slot_token = jnp.where(
        jnp.any(matches, axis=1),
        jnp.sum(jnp.where(matches, pair_token[None, :], 0), axis=1),
        tok_count,
    )
    padded_tokens = jnp.concatenate([tokens, jnp.zeros((1, feat_local), tokens.dtype)], axis=0)
    send_rows = padded_tokens[slot_token].reshape(group_count, member_count, capacity * feat_local)
    arrived = lax.all_to_all(
        lax.all_to_all(send_rows, "node", split_axis=0, concat_axis=0, tiled=True),
        "local",
        split_axis=1,
        concat_axis=1,
        tiled=True,
    )
    routed_rows = arrived.reshape(slot_total, feat_local)
    stacked = jnp.concatenate([routed_rows, tokens], axis=0)
    segment = lax.all_gather(stacked, "ctx", axis=1, tiled=True)
    routed_part = segment[:slot_total]
    shared_part = segment[slot_total:]
    gate_routed = matmul(routed_part, gate_local)
    up_routed = matmul(routed_part, up_local)
    gate_shared = matmul(shared_part, shared_gate)
    up_shared = matmul(shared_part, shared_up)
    routed_hidden = (jax.nn.silu(gate_routed) * up_routed).astype(jnp.bfloat16)
    shared_hidden = (jax.nn.silu(gate_shared) * up_shared).astype(jnp.bfloat16)
    hidden_stack = jnp.concatenate([routed_hidden, shared_hidden], axis=0)
    segment = lax.all_gather(hidden_stack, "ctx", axis=1, tiled=True)
    routed_out = matmul(segment[:slot_total], down_local)
    shared_out = matmul(segment[slot_total:], shared_down)
    routed_bf = routed_out.astype(jnp.bfloat16)
    sendback = routed_bf.reshape(group_count, member_count, capacity * out_width)
    returned = lax.all_to_all(
        lax.all_to_all(sendback, "node", split_axis=0, concat_axis=0, tiled=True),
        "local",
        split_axis=1,
        concat_axis=1,
        tiled=True,
    )
    returned = returned.reshape(slot_total, out_width)
    pair_out = returned[pair_slot].reshape(tok_count, top_count, out_width).astype(jnp.float32)
    weighted = gate_weights[:, :, None] * pair_out
    group_sum = jnp.einsum(
        "tkg,tkd->tgd", group_onehot.astype(jnp.float32), weighted, precision=lax.Precision.HIGHEST
    )
    rounded = lax.optimization_barrier(group_sum.astype(jnp.bfloat16)).astype(jnp.float32)
    routed_sum = jnp.sum(rounded, axis=1)
    mixed = shared_out + routed_sum
    return mixed.astype(jnp.bfloat16)


def column_tiles(width, tile, visit):
    whole = width // tile
    if whole == 1:
        visit(0, tile)
    elif whole > 1:

        def step(index, carry):
            visit(pl.multiple_of(index * tile, tile), tile)
            return carry

        lax.fori_loop(0, whole, step, 0)
    if width % tile:
        visit(whole * tile, width % tile)


def cube_kernel(
    sizes,
    tok_in,
    ids_in,
    scores_in,
    wg_in,
    wu_in,
    wd_in,
    sg_in,
    su_in,
    sd_in,
    out_ref,
    tok,
    meta,
    wg,
    wu,
    wd,
    sg,
    su,
    sd,
    rows_in,
    hid_s,
    hid,
    part,
    got,
    total,
    sum_g,
    sum_u,
    hold,
    loc_sem,
    z_send,
    z_recv,
    b_send,
    b_recv,
    m_send,
    m_recv,
    p_send,
    p_recv,
):
    ctx_count, group_count, member_count, cap = sizes
    c = lax.axis_index("ctx")
    n = lax.axis_index("node")
    l = lax.axis_index("local")
    last = ctx_count - 1
    tok_count = tok.shape[2]
    feat = tok.shape[3]
    width = wg.shape[1]
    out_width = wd.shape[1]
    slots = range(1, tok.shape[0])

    def peer(slot):
        node = n
        if slot & 1:
            node = node + 1 - 2 * lax.rem(node, 2)
        if slot & 4:
            node = lax.rem(node + group_count // 2, group_count)
        member = lax.rem(l + 1, member_count) if slot & 2 else l
        return {"node": node, "local": member}

    first = pltpu.make_async_copy(tok_in, tok.at[0, c], loc_sem.at[0])
    first.start()

    barrier = pltpu.get_barrier_semaphore()
    for slot in slots:
        pl.semaphore_signal(barrier, inc=1, device_id=peer(slot), device_id_type=MESH)

    @pl.when(c > 0)
    def _():
        pl.semaphore_signal(barrier, inc=1, device_id={"ctx": c - 1}, device_id_type=MESH)

    @pl.when(c < last)
    def _():
        pl.semaphore_signal(barrier, inc=1, device_id={"ctx": c + 1}, device_id_type=MESH)

    loads = []
    for index, (src, dst) in enumerate(
        ((sg_in, sg), (su_in, su), (wg_in, wg), (wu_in, wu), (sd_in, sd), (wd_in, wd))
    ):
        loads.append(pltpu.make_async_copy(src, dst, loc_sem.at[2 + index]))

    inner = (c > 0) & (c < last)

    @pl.when(inner)
    def _():
        pl.semaphore_wait(barrier, len(slots) + 2)

    @pl.when(jnp.logical_not(inner))
    def _():
        pl.semaphore_wait(barrier, len(slots) + 1)

    first.wait()

    def piece(chunk, shard):
        if chunk == 0:
            return tok.at[0, shard]
        if chunk == 1:
            return hid_s.at[shard]
        return hid.at[chunk - 2, shard]

    def line(chunk, depth, way, shard, target):
        return pltpu.make_async_remote_copy(
            src_ref=piece(chunk, shard),
            dst_ref=piece(chunk, shard),
            send_sem=z_send.at[way, depth, chunk],
            recv_sem=z_recv.at[way, depth, chunk],
            device_id={"ctx": target},
            device_id_type=MESH,
        )

    def line_send(chunk, depth, finish=False):
        for way in (0, 1):
            shard, target = (c - depth, c + 1) if way == 0 else (c + depth, c - 1)
            ready = (c >= depth) & (c < last) if way == 0 else (c + depth <= last) & (c > 0)

            @pl.when(ready)
            def _():
                copy = line(chunk, depth, way, shard, target)
                if finish:
                    copy.wait_send()
                else:
                    copy.start()

    def line_take(chunk, depth, then=None):
        for way in (0, 1):
            shard = c - 1 - depth if way == 0 else c + 1 + depth
            ready = shard >= 0 if way == 0 else shard <= last

            @pl.when(ready)
            def _():
                source = c - 1 if way == 0 else c + 1
                line(chunk, depth, way, shard, source).wait_recv()
                target = c + 1 if way == 0 else c - 1
                if depth < last - 1:

                    @pl.when(target < ctx_count if way == 0 else target >= 0)
                    def _():
                        line(chunk, depth + 1, way, shard, target).start()

                if then is not None:
                    then(shard)

    def hand(src_slot, dst_slot, shard, over):
        return pltpu.make_async_remote_copy(
            src_ref=tok.at[src_slot, shard],
            dst_ref=tok.at[dst_slot, shard],
            send_sem=b_send.at[dst_slot, shard],
            recv_sem=b_recv.at[dst_slot, shard],
            device_id=peer(over),
            device_id_type=MESH,
        )

    def spread(shard):
        hand(0, 2, shard, 2).start()
        hand(0, 4, shard, 4).start()
        hand(0, 1, shard, 1).start()

    line_send(0, 0)
    spread(c)
    for load in loads:
        load.start()

    scores = scores_in[...]
    scaled = route_scale * scores / jnp.sum(scores, axis=0, keepdims=True)
    gates = scaled.astype(jnp.bfloat16).astype(jnp.float32)
    row = lax.broadcasted_iota(jnp.int32, meta.shape[1:], 0)
    named = jnp.zeros(row.shape, jnp.float32)
    table = jnp.zeros(row.shape, jnp.float32)
    for k in range(ids_in.shape[0]):
        expert = ids_in[k : k + 1, :]
        named = jnp.where(row == expert // member_count, 1.0, named)
        table = table + jnp.where(row == expert + group_count, gates[k : k + 1, :], 0.0)
    square = (tok_count, tok_count)
    before = lax.broadcasted_iota(jnp.int32, square, 0) < lax.broadcasted_iota(jnp.int32, square, 1)
    counts = matmul(named.astype(jnp.bfloat16), jnp.where(before, 1.0, 0.0).astype(jnp.bfloat16))
    meta[0] = jnp.where(row < group_count, jnp.where(named > 0.5, counts, -1.0), table)

    greet = []
    for slot in slots:
        greet.append(
            pltpu.make_async_remote_copy(
                src_ref=meta.at[0],
                dst_ref=meta.at[slot],
                send_sem=m_send.at[slot],
                recv_sem=m_recv.at[slot],
                device_id=peer(slot),
                device_id_type=MESH,
            )
        )
        greet[-1].start()

    def shared_add(shard, fresh=False):
        ins = pl.ds(pl.multiple_of(shard * feat, 128), feat)

        def visit(start, size):
            cols = pl.ds(start, size)
            g = matmul(tok[0, shard], sg[ins, cols])
            u = matmul(tok[0, shard], su[ins, cols])
            sum_g[:, cols] = g if fresh else sum_g[:, cols] + g
            sum_u[:, cols] = u if fresh else sum_u[:, cols] + u

        column_tiles(width, 256, visit)

    loads[0].wait()
    loads[1].wait()
    shared_add(c, True)
    for depth in range(last):
        line_take(0, depth, spread)
        for shard in (c - 1 - depth, c + 1 + depth):

            @pl.when((shard >= 0) & (shard <= last))
            def _():
                shared_add(shard)


    rank_of = lambda slot: meta[slot, pl.ds(n, 1), :]
    weight_of = lambda slot: meta[slot, pl.ds(group_count + n * member_count + l, 1), :]

    def pick(row, slot):
        spots = lax.broadcasted_iota(jnp.int32, (cap, tok_count), 0).astype(jnp.float32)
        mask = jnp.where(spots == rank_of(slot), 1.0, 0.0).astype(jnp.bfloat16)

        def step(shard, carry):
            chosen = matmul(mask, tok[slot, shard]).astype(jnp.bfloat16)
            rows_in[row : row + cap, pl.ds(pl.multiple_of(shard * feat, 128), feat)] = chosen
            return carry

        lax.fori_loop(0, ctx_count, step, 0)

    def hidden(count, gate, up, target):
        def visit(start, size):
            cols = pl.ds(start, size)
            g = matmul(rows_in[0:count, :], gate[:, cols])
            u = matmul(rows_in[0:count, :], up[:, cols])
            target[:, cols] = (g / (1.0 + jnp.exp(-g)) * u).astype(jnp.bfloat16)

        column_tiles(width, 256, visit)

    pairs = ((2, 3), (4, 5), (6, 7), (0, 1))

    def compute(index):
        for place, slot in enumerate(pairs[index]):
            pick(place * cap, slot)
        hidden(2 * cap, wg, wu, hid.at[index, c])

    half = ctx_count // 2

    def take(slot, shard):
        hand(0, slot, shard, 1).wait_recv()

    g = sum_g[...]
    hid_s[c] = (g / (1.0 + jnp.exp(-g)) * sum_u[...]).astype(jnp.bfloat16)
    line_send(1, 0)

    for copy in greet:
        copy.wait_recv()
    loads[2].wait()
    loads[3].wait()
    for shard in range(ctx_count):
        take(1, shard)
    compute(3)
    line_send(5, 0)
    line_take(1, 0)
    for shard in range(ctx_count):
        take(2, shard)
        hand(2, 3, shard, 1).start()
        if shard < half:
            hand(2, 6, shard, 4).start()
        take(4, shard)
        hand(4, 5, shard, 1).start()
        if shard >= half:
            hand(4, 6, shard, 2).start()
    for shard in range(ctx_count):
        take(3, shard)
    compute(0)
    line_send(2, 0)
    line_take(1, 1)
    for shard in range(ctx_count):
        take(5, shard)
    compute(1)
    line_send(3, 0)
    line_take(2, 0)
    line_take(1, 2)

    loads[4].wait()
    loads[5].wait()

    def product(chunk, down, cols):
        value = matmul(piece(chunk, 0)[...], down[0:width, cols])
        for shard in range(1, ctx_count):
            value = value + matmul(
                piece(chunk, shard)[...], down[shard * width : (shard + 1) * width, cols]
            )
        return value

    def shared_down(start, size):
        cols = pl.ds(start, size)
        total[:, cols] = product(1, sd, cols)

    column_tiles(out_width, 256, shared_down)

    sends = {}

    def ship(slot, over):
        sends[slot] = pltpu.make_async_remote_copy(
            src_ref=part.at[slot - 1],
            dst_ref=got.at[slot - 1],
            send_sem=p_send.at[slot],
            recv_sem=p_recv.at[slot],
            device_id=peer(over),
            device_id_type=MESH,
        )
        sends[slot].start()

    def finish(index):
        weights = []
        for slot in pairs[index]:
            spots = lax.broadcasted_iota(jnp.int32, (tok_count, tok_count), 0).astype(jnp.float32)
            mask = jnp.where(spots == rank_of(slot), weight_of(slot), 0.0)
            weights.append(jnp.transpose(mask)[:, 0:cap].astype(jnp.bfloat16))

        def visit(start, size):
            cols = pl.ds(start, size)
            rows = product(index + 2, wd, cols).astype(jnp.bfloat16)
            for place, slot in enumerate(pairs[index]):
                value = matmul(weights[place], rows[place * cap : (place + 1) * cap])
                if slot == 0:
                    total[:, cols] += value
                elif place == 0:
                    hold[:, cols] = value
                else:
                    part[slot - 1, :, cols] = value.astype(jnp.bfloat16)

        column_tiles(out_width, 256, visit)
        ship(pairs[index][1], 1)

    def forward(index):
        slot, other = pairs[index]
        sends[other].wait_recv()

        def visit(start, size):
            cols = pl.ds(start, size)
            value = hold[:, cols] + got[other - 1, :, cols].astype(jnp.float32)
            part[slot - 1, :, cols] = value.astype(jnp.bfloat16)

        column_tiles(out_width, 256, visit)
        ship(slot, slot)

    for shard in range(ctx_count):
        take(6, shard)
        hand(6, 7, shard, 1).start()
    line_take(2, 1)
    for shard in range(ctx_count):
        take(7, shard)
    compute(2)
    line_send(4, 0)
    line_take(3, 0)
    line_take(3, 1)
    line_take(2, 2)
    finish(0)
    line_take(4, 0)
    forward(0)
    line_take(4, 1)
    line_take(3, 2)
    finish(1)
    line_take(5, 0)
    forward(1)
    line_take(5, 1)
    line_take(4, 2)
    finish(2)
    forward(2)
    for slot in (2, 4):
        sends[slot].wait_recv()

    def gather_some(start, size):
        cols = pl.ds(start, size)
        value = total[:, cols]
        for slot in (2, 4):
            value = value + got[slot - 1, :, cols].astype(jnp.float32)
        total[:, cols] = value

    column_tiles(out_width, 256, gather_some)
    line_take(5, 2)
    finish(3)
    for slot in (6, 1):
        sends[slot].wait_recv()

    def gather_rest(start, size):
        cols = pl.ds(start, size)
        value = total[:, cols]
        for slot in (6, 1):
            value = value + got[slot - 1, :, cols].astype(jnp.float32)
        out_ref[:, cols] = value.astype(jnp.bfloat16)

    column_tiles(out_width, 256, gather_rest)

    for copy in list(sends.values()) + greet:
        copy.wait_send()
    for chunk in range(6):
        for depth in range(last):
            line_send(chunk, depth, finish=True)
    for shard in range(ctx_count):
        for slot in (1, 2, 3, 4, 5, 6, 7):
            hand(0, slot, shard, 1).wait_send()


def cube(
    tokens, expert_ids, route_scores, w_gate, w_up, w_down, shared_gate, shared_up, shared_down
):
    ctx_count = lax.axis_size("ctx")
    group_count = lax.axis_size("node")
    member_count = lax.axis_size("local")
    expert_count = group_count * member_count
    tok_count, feat = tokens.shape
    cap = (10 * tok_count + 4 * group_count - 1) // (4 * group_count)
    hidden_units, out_width = w_down.shape[1:]
    width = w_gate.shape[2]
    meta_rows = -(-(group_count + expert_count) // 16) * 16
    slots = 2 * group_count
    bf16 = jnp.bfloat16
    rows = max(2 * cap, tok_count)
    anywhere = pl.BlockSpec(memory_space=pl.ANY)
    inside = pl.BlockSpec(memory_space=pltpu.VMEM)
    dma = pltpu.SemaphoreType.DMA
    kernel = lambda *refs: cube_kernel((ctx_count, group_count, member_count, cap), *refs)
    return pl.pallas_call(
        kernel,
        out_shape=jax.ShapeDtypeStruct((tok_count, out_width), bf16),
        in_specs=[anywhere, inside, inside] + [anywhere] * 6,
        out_specs=inside,
        scratch_shapes=[
            pltpu.VMEM((slots, ctx_count, tok_count, feat), bf16),
            pltpu.VMEM((slots, meta_rows, tok_count), jnp.float32),
            pltpu.VMEM(w_gate.shape[1:], bf16),
            pltpu.VMEM(w_up.shape[1:], bf16),
            pltpu.VMEM(w_down.shape[1:], bf16),
            pltpu.VMEM(shared_gate.shape, bf16),
            pltpu.VMEM(shared_up.shape, bf16),
            pltpu.VMEM(shared_down.shape, bf16),
            pltpu.VMEM((rows, ctx_count * feat), bf16),
            pltpu.VMEM((ctx_count, tok_count, width), bf16),
            pltpu.VMEM((4, ctx_count, 2 * cap, width), bf16),
            pltpu.VMEM((slots - 1, tok_count, out_width), bf16),
            pltpu.VMEM((slots - 1, tok_count, out_width), bf16),
            pltpu.VMEM((tok_count, out_width), jnp.float32),
            pltpu.VMEM((tok_count, width), jnp.float32),
            pltpu.VMEM((tok_count, width), jnp.float32),
            pltpu.VMEM((tok_count, out_width), jnp.float32),
            dma((8,)),
            dma((2, ctx_count - 1, 6)),
            dma((2, ctx_count - 1, 6)),
            dma((slots, ctx_count)),
            dma((slots, ctx_count)),
            dma((slots,)),
            dma((slots,)),
            dma((slots,)),
            dma((slots,)),
        ],
        compiler_params=pltpu.CompilerParams(
            collective_id=0, has_side_effects=True, vmem_limit_bytes=VMEM_BYTES
        ),
    )(
        tokens,
        expert_ids.T,
        route_scores.T,
        w_gate[0],
        w_up[0],
        w_down[0],
        shared_gate,
        shared_up,
        shared_down,
    )


def local(tokens, expert_ids, *rest):
    whole_groups = expert_ids.shape[1] == 2 * lax.axis_size("local")
    if whole_groups and lax.axis_size("local") == 2 and lax.axis_size("node") == 4:
        return cube(tokens, expert_ids, *rest)
    return exchange(tokens, expert_ids, *rest)


def solution(mesh):
    return jax.shard_map(
        local,
        mesh=mesh,
        in_specs=(
            P(("node", "local"), "ctx"),
            P(("node", "local"), None),
            P(("node", "local"), None),
            P(("node", "local"), None, "ctx"),
            P(("node", "local"), None, "ctx"),
            P(("node", "local"), None, "ctx"),
            P(None, "ctx"),
            P(None, "ctx"),
            P(None, "ctx"),
        ),
        out_specs=P(("node", "local"), "ctx"),
        check_vma=False,
    )
```

profile of v0, /device:TPU:0, one launch (start us, length us, event | category | flops | bytes accessed | tf_op | source)
XLA Modules:
  0.0 88.5 jit_solution(8025120810991640517)
XLA Ops:
  0.0 86.9 %shard_map.91 = bf16[128,896]{1,0:T(8,128)(2,1)} custom-call(bf16[128,896]{1,0:T(8,128)(2,1)} %refs_0_.1, s32[4,128]{1,0:T(4,128)} %bitcast.8, f32[4,128]{1,0:T(4,128)} %bitcast.9, bf16[3584,512]{1,0:T(8,128)(2,1)} %bitcast.5, bf16[3584,512]{1,0:T(8,128)(2,1)} %bitcast.6, bf16[2048,896]{1,0:T(8,128)(2,1)} %bitcast.7, bf16[3584,512]{1,0:T(8,128)(2,1)} %refs_6_.1, ...), custom_call_target="tpu_custom_call" | custom-call | tf_op jit(solution)/shard_map/pallas_call | solution.py:536
  86.9 1.6 %copy.11 = bf16[128,896]{1,0:T(8,128)(2,1)} copy(bf16[128,896]{1,0:T(8,128)(2,1)} %shard_map.91) | data formatting | bytes 458752
where the time goes:
time: 89 us; the launch traced here: 88.5 us
  Pallas kernels  86.9 us (98%)
  local copies, waits for them, and re-layouts  1.65 us (2%)
    pallas_call x1, Pallas kernels, cube(): pl.pallas_call(kernel, out_shape=jax.ShapeDtypeStruct((tok_count, out_wid...  86.9 us

commit v1 on v0

--- a/solution.py
+++ b/solution.py
@@ -137,6 +137,8 @@
     total,
     sum_g,
     sum_u,
+    acc_g,
+    acc_u,
     hold,
     loc_sem,
     z_send,
@@ -170,25 +172,27 @@
 
     first = pltpu.make_async_copy(tok_in, tok.at[0, c], loc_sem.at[0])
     first.start()
-
-    barrier = pltpu.get_barrier_semaphore()
-    for slot in slots:
-        pl.semaphore_signal(barrier, inc=1, device_id=peer(slot), device_id_type=MESH)
-
-    @pl.when(c > 0)
-    def _():
-        pl.semaphore_signal(barrier, inc=1, device_id={"ctx": c - 1}, device_id_type=MESH)
-
-    @pl.when(c < last)
-    def _():
-        pl.semaphore_signal(barrier, inc=1, device_id={"ctx": c + 1}, device_id_type=MESH)
-
     loads = []
     for index, (src, dst) in enumerate(
         ((sg_in, sg), (su_in, su), (wg_in, wg), (wu_in, wu), (sd_in, sd), (wd_in, wd))
     ):
         loads.append(pltpu.make_async_copy(src, dst, loc_sem.at[2 + index]))
 
+    barrier = pltpu.get_barrier_semaphore()
+    for slot in slots:
+        pl.semaphore_signal(barrier, inc=1, device_id=peer(slot), device_id_type=MESH)
+
+    @pl.when(c > 0)
+    def _():
+        pl.semaphore_signal(barrier, inc=1, device_id={"ctx": c - 1}, device_id_type=MESH)
+
+    @pl.when(c < last)
+    def _():
+        pl.semaphore_signal(barrier, inc=1, device_id={"ctx": c + 1}, device_id_type=MESH)
+
+    for load in loads:
+        load.start()
+
     inner = (c > 0) & (c < last)
 
     @pl.when(inner)
@@ -201,12 +205,16 @@
 
     first.wait()
 
+    SHARED = 2
+    PAIR = 3
+    half_rows = tok_count // 2
+
     def piece(chunk, shard):
-        if chunk == 0:
-            return tok.at[0, shard]
-        if chunk == 1:
+        if chunk < 2:
+            return tok.at[0, shard, pl.ds(chunk * half_rows, half_rows)]
+        if chunk == SHARED:
             return hid_s.at[shard]
-        return hid.at[chunk - 2, shard]
+        return hid.at[chunk - PAIR, shard]
 
     def line(chunk, depth, way, shard, target):
         return pltpu.make_async_remote_copy(
@@ -231,24 +239,43 @@
                 else:
                     copy.start()
 
-    def line_take(chunk, depth, then=None):
+    def line_take(chunk, depth, relays, then=None):
         for way in (0, 1):
             shard = c - 1 - depth if way == 0 else c + 1 + depth
-            ready = shard >= 0 if way == 0 else shard <= last
-
-            @pl.when(ready)
+            source = c - 1 if way == 0 else c + 1
+            target = c + 1 if way == 0 else c - 1
+            here = shard >= 0 if way == 0 else shard <= last
+            passes = target < ctx_count if way == 0 else target >= 0
+            if depth == last - 1:
+                if relays:
+                    continue
+            else:
+                here = here & (passes if relays else jnp.logical_not(passes))
+
+            @pl.when(here)
             def _():
-                source = c - 1 if way == 0 else c + 1
                 line(chunk, depth, way, shard, source).wait_recv()
-                target = c + 1 if way == 0 else c - 1
-                if depth < last - 1:
-
-                    @pl.when(target < ctx_count if way == 0 else target >= 0)
-                    def _():
-                        line(chunk, depth + 1, way, shard, target).start()
-
+                if relays:
+                    line(chunk, depth + 1, way, shard, target).start()
                 if then is not None:
                     then(shard)
+
+    def relay_line(chunk, depth, then=None):
+        line_take(chunk, depth, True, then)
+
+    def await_line(chunk):
+        for depth in range(last):
+            line_take(chunk, depth, False)
+
+    def at_stage(stage, then):
+        if stage == 0:
+            then(c)
+            return
+        for shard in (c - stage, c + stage):
+
+            @pl.when((shard >= 0) & (shard <= last))
+            def _():
+                then(shard)
 
     def hand(src_slot, dst_slot, shard, over):
         return pltpu.make_async_remote_copy(
@@ -261,14 +288,15 @@
         )
 
     def spread(shard):
+        hand(0, 1, shard, 1).start()
         hand(0, 2, shard, 2).start()
         hand(0, 4, shard, 4).start()
-        hand(0, 1, shard, 1).start()
+
+    def take(slot, shard):
+        hand(0, slot, shard, 1).wait_recv()
 
     line_send(0, 0)
-    spread(c)
-    for load in loads:
-        load.start()
+    line_send(1, 0)
 
     scores = scores_in[...]
     scaled = route_scale * scores / jnp.sum(scores, axis=0, keepdims=True)
@@ -298,9 +326,13 @@
             )
         )
         greet[-1].start()
+    spread(c)
+
+    def columns(shard):
+        return pl.ds(pl.multiple_of(shard * feat, 128), feat)
 
     def shared_add(shard, fresh=False):
-        ins = pl.ds(pl.multiple_of(shard * feat, 128), feat)
+        ins = columns(shard)
 
         def visit(start, size):
             cols = pl.ds(start, size)
@@ -311,28 +343,34 @@
 
         column_tiles(width, 256, visit)
 
-    loads[0].wait()
-    loads[1].wait()
-    shared_add(c, True)
-    for depth in range(last):
-        line_take(0, depth, spread)
-        for shard in (c - 1 - depth, c + 1 + depth):
-
-            @pl.when((shard >= 0) & (shard <= last))
-            def _():
-                shared_add(shard)
-
-
     rank_of = lambda slot: meta[slot, pl.ds(n, 1), :]
     weight_of = lambda slot: meta[slot, pl.ds(group_count + n * member_count + l, 1), :]
 
+    def mask_of(slot):
+        spots = lax.broadcasted_iota(jnp.int32, (cap, tok_count), 0).astype(jnp.float32)
+        return jnp.where(spots == rank_of(slot), 1.0, 0.0).astype(jnp.bfloat16)
+
+    def pair_add(shard, fresh=False):
+        ins = columns(shard)
+        for place, slot in enumerate(pairs[3]):
+            chosen = matmul(mask_of(slot), tok[slot, shard]).astype(jnp.bfloat16)
+            rows_in[place * cap : (place + 1) * cap, ins] = chosen
+
+        def visit(start, size):
+            cols = pl.ds(start, size)
+            g = matmul(rows_in[0 : 2 * cap, ins], wg[ins, cols])
+            u = matmul(rows_in[0 : 2 * cap, ins], wu[ins, cols])
+            acc_g[:, cols] = g if fresh else acc_g[:, cols] + g
+            acc_u[:, cols] = u if fresh else acc_u[:, cols] + u
+
+        column_tiles(width, 256, visit)
+
     def pick(row, slot):
-        spots = lax.broadcasted_iota(jnp.int32, (cap, tok_count), 0).astype(jnp.float32)
-        mask = jnp.where(spots == rank_of(slot), 1.0, 0.0).astype(jnp.bfloat16)
+        mask = mask_of(slot)
 
         def step(shard, carry):
             chosen = matmul(mask, tok[slot, shard]).astype(jnp.bfloat16)
-            rows_in[row : row + cap, pl.ds(pl.multiple_of(shard * feat, 128), feat)] = chosen
+            rows_in[row : row + cap, columns(shard)] = chosen
             return carry
 
         lax.fori_loop(0, ctx_count, step, 0)
@@ -355,72 +393,116 @@
 
     half = ctx_count // 2
 
-    def take(slot, shard):
-        hand(0, slot, shard, 1).wait_recv()
-
+    loads[0].wait()
+    loads[1].wait()
+    shared_add(c, True)
+    greet[0].wait_recv()
+    loads[2].wait()
+    loads[3].wait()
+    take(1, c)
+    pair_add(c, True)
+
+    def both_add(shard):
+        shared_add(shard)
+        take(1, shard)
+        pair_add(shard)
+
+    for depth in range(last):
+        for chunk, then in ((0, None), (1, spread)):
+            for relays in (True, False):
+                line_take(chunk, depth, relays, then)
+        at_stage(depth + 1, both_add)
+
+    g = acc_g[...]
+    hid[3, c] = (g / (1.0 + jnp.exp(-g)) * acc_u[...]).astype(jnp.bfloat16)
+    line_send(PAIR + 3, 0)
     g = sum_g[...]
     hid_s[c] = (g / (1.0 + jnp.exp(-g)) * sum_u[...]).astype(jnp.bfloat16)
-    line_send(1, 0)
-
-    for copy in greet:
-        copy.wait_recv()
-    loads[2].wait()
-    loads[3].wait()
-    for shard in range(ctx_count):
-        take(1, shard)
-    compute(3)
-    line_send(5, 0)
-    line_take(1, 0)
-    for shard in range(ctx_count):
+    line_send(SHARED, 0)
+
+    def relay(shard):
         take(2, shard)
         hand(2, 3, shard, 1).start()
-        if shard < half:
+
+        @pl.when(shard < half)
+        def _():
             hand(2, 6, shard, 4).start()
+
         take(4, shard)
         hand(4, 5, shard, 1).start()
-        if shard >= half:
+
+        @pl.when(shard >= half)
+        def _():
             hand(4, 6, shard, 2).start()
+
+    at_stage(0, relay)
+    at_stage(1, relay)
+    relay_line(PAIR + 3, 0)
+    for stage in range(2, ctx_count):
+        at_stage(stage, relay)
+    for copy in greet[1:]:
+        copy.wait_recv()
     for shard in range(ctx_count):
         take(3, shard)
     compute(0)
-    line_send(2, 0)
-    line_take(1, 1)
+    line_send(PAIR, 0)
     for shard in range(ctx_count):
         take(5, shard)
     compute(1)
-    line_send(3, 0)
-    line_take(2, 0)
-    line_take(1, 2)
+    line_send(PAIR + 1, 0)
+    relay_line(PAIR + 3, 1)
+    for shard in range(ctx_count):
+        take(6, shard)
+        hand(6, 7, shard, 1).start()
+    relay_line(PAIR, 0)
+    relay_line(PAIR + 1, 0)
+    for shard in range(ctx_count):
+        take(7, shard)
+    compute(2)
+    line_send(PAIR + 2, 0)
+    relay_line(PAIR, 1)
 
     loads[4].wait()
     loads[5].wait()
 
-    def product(chunk, down, cols):
-        value = matmul(piece(chunk, 0)[...], down[0:width, cols])
+    def product(index, down, cols):
+        value = matmul(hid[index, 0], down[0:width, cols])
         for shard in range(1, ctx_count):
             value = value + matmul(
-                piece(chunk, shard)[...], down[shard * width : (shard + 1) * width, cols]
+                hid[index, shard], down[shard * width : (shard + 1) * width, cols]
             )
         return value
 
-    def shared_down(start, size):
-        cols = pl.ds(start, size)
-        total[:, cols] = product(1, sd, cols)
-
-    column_tiles(out_width, 256, shared_down)
-
+    def shared_out(shard, fresh=False):
+        units = pl.ds(pl.multiple_of(shard * width, 128), width)
+
+        def visit(start, size):
+            cols = pl.ds(start, size)
+            value = matmul(hid_s[shard], sd[units, cols])
+            total[:, cols] = value if fresh else total[:, cols] + value
+
+        column_tiles(out_width, 256, visit)
+
+    split = -(-out_width // 256) * 128
+    parts = ((0, split), (split, out_width - split))
     sends = {}
 
-    def ship(slot, over):
-        sends[slot] = pltpu.make_async_remote_copy(
-            src_ref=part.at[slot - 1],
-            dst_ref=got.at[slot - 1],
-            send_sem=p_send.at[slot],
-            recv_sem=p_recv.at[slot],
+    def ship(slot, over, part_index):
+        cols = pl.ds(*parts[part_index])
+        copy = pltpu.make_async_remote_copy(
+            src_ref=part.at[slot - 1, :, cols],
+            dst_ref=got.at[slot - 1, :, cols],
+            send_sem=p_send.at[slot, part_index],
+            recv_sem=p_recv.at[slot, part_index],
             device_id=peer(over),
             device_id_type=MESH,
         )
-        sends[slot].start()
+        sends[slot, part_index] = copy
+        copy.start()
+
+    def tiles(part_index, visit):
+        begin, size = parts[part_index]
+        column_tiles(size, 256, lambda start, count: visit(begin + start, count))
 
     def finish(index):
         weights = []
@@ -430,8 +512,8 @@
             weights.append(jnp.transpose(mask)[:, 0:cap].astype(jnp.bfloat16))
 
         def visit(start, size):
-            cols = pl.ds(start, size)
-            rows = product(index + 2, wd, cols).astype(jnp.bfloat16)
+            cols = pl.ds(start if isinstance(start, int) else pl.multiple_of(start, 128), size)
+            rows = product(index, wd, cols).astype(jnp.bfloat16)
             for place, slot in enumerate(pairs[index]):
                 value = matmul(weights[place], rows[place * cap : (place + 1) * cap])
                 if slot == 0:
@@ -441,72 +523,68 @@
                 else:
                     part[slot - 1, :, cols] = value.astype(jnp.bfloat16)
 
-        column_tiles(out_width, 256, visit)
-        ship(pairs[index][1], 1)
+        for part_index in range(2):
+            tiles(part_index, visit)
+            ship(pairs[index][1], 1, part_index)
 
     def forward(index):
         slot, other = pairs[index]
-        sends[other].wait_recv()
 
         def visit(start, size):
-            cols = pl.ds(start, size)
+            cols = pl.ds(start if isinstance(start, int) else pl.multiple_of(start, 128), size)
             value = hold[:, cols] + got[other - 1, :, cols].astype(jnp.float32)
             part[slot - 1, :, cols] = value.astype(jnp.bfloat16)
 
-        column_tiles(out_width, 256, visit)
-        ship(slot, slot)
-
-    for shard in range(ctx_count):
-        take(6, shard)
-        hand(6, 7, shard, 1).start()
-    line_take(2, 1)
-    for shard in range(ctx_count):
-        take(7, shard)
-    compute(2)
-    line_send(4, 0)
-    line_take(3, 0)
-    line_take(3, 1)
-    line_take(2, 2)
+        for part_index in range(2):
+            sends[other, part_index].wait_recv()
+            tiles(part_index, visit)
+            ship(slot, slot, part_index)
+
+    shared_out(c, True)
+    await_line(PAIR + 3)
+    finish(3)
+    relay_line(PAIR + 1, 1)
+    relay_line(PAIR + 2, 0)
+    relay_line(PAIR + 2, 1)
+    relay_line(SHARED, 0)
+    relay_line(SHARED, 1)
+    await_line(PAIR)
     finish(0)
-    line_take(4, 0)
     forward(0)
-    line_take(4, 1)
-    line_take(3, 2)
+    await_line(PAIR + 1)
     finish(1)
-    line_take(5, 0)
     forward(1)
-    line_take(5, 1)
-    line_take(4, 2)
+    await_line(PAIR + 2)
     finish(2)
     forward(2)
-    for slot in (2, 4):
-        sends[slot].wait_recv()
 
     def gather_some(start, size):
         cols = pl.ds(start, size)
         value = total[:, cols]
-        for slot in (2, 4):
+        for slot in (1, 2, 4):
             value = value + got[slot - 1, :, cols].astype(jnp.float32)
         total[:, cols] = value
 
+    for slot in (1, 2, 4):
+        for part_index in range(2):
+            sends[slot, part_index].wait_recv()
     column_tiles(out_width, 256, gather_some)
-    line_take(5, 2)
-    finish(3)
-    for slot in (6, 1):
-        sends[slot].wait_recv()
+    await_line(SHARED)
+    for depth in range(last):
+        at_stage(depth + 1, shared_out)
 
     def gather_rest(start, size):
-        cols = pl.ds(start, size)
-        value = total[:, cols]
-        for slot in (6, 1):
-            value = value + got[slot - 1, :, cols].astype(jnp.float32)
+        cols = pl.ds(start if isinstance(start, int) else pl.multiple_of(start, 128), size)
+        value = total[:, cols] + got[5, :, cols].astype(jnp.float32)
         out_ref[:, cols] = value.astype(jnp.bfloat16)
 
-    column_tiles(out_width, 256, gather_rest)
+    for part_index in range(2):
+        sends[6, part_index].wait_recv()
+        tiles(part_index, gather_rest)
 
     for copy in list(sends.values()) + greet:
         copy.wait_send()
-    for chunk in range(6):
+    for chunk in range(PAIR + 4):
         for depth in range(last):
             line_send(chunk, depth, finish=True)
     for shard in range(ctx_count):
@@ -555,16 +633,18 @@
             pltpu.VMEM((tok_count, out_width), jnp.float32),
             pltpu.VMEM((tok_count, width), jnp.float32),
             pltpu.VMEM((tok_count, width), jnp.float32),
+            pltpu.VMEM((2 * cap, width), jnp.float32),
+            pltpu.VMEM((2 * cap, width), jnp.float32),
             pltpu.VMEM((tok_count, out_width), jnp.float32),
             dma((8,)),
-            dma((2, ctx_count - 1, 6)),
-            dma((2, ctx_count - 1, 6)),
+            dma((2, ctx_count - 1, 7)),
+            dma((2, ctx_count - 1, 7)),
             dma((slots, ctx_count)),
             dma((slots, ctx_count)),
             dma((slots,)),
             dma((slots,)),
-            dma((slots,)),
-            dma((slots,)),
+            dma((slots, 2)),
+            dma((slots, 2)),
         ],
         compiler_params=pltpu.CompilerParams(
             collective_id=0, has_side_effects=True, vmem_limit_bytes=VMEM_BYTES

time: 89 us -> 85.9 us (0.965)
  Pallas kernels: 86.9 us -> 84.1 us
    pallas_call x1, Pallas kernels: 86.9 us -> 84.1 us  [cube(): pl.pallas_call(kernel, out_shape=jax.ShapeDtypeStruct((tok_count, out_wid...]
where the time goes in v1:
time: 85.9 us; the launch traced here: 85.7 us
  Pallas kernels  84.1 us (98%)
  local copies, waits for them, and re-layouts  1.65 us (2%)
    pallas_call x1, Pallas kernels, cube(): pl.pallas_call(kernel, out_shape=jax.ShapeDtypeStruct((tok_count, out_wid...  84.1 us

profile of v1, /device:TPU:0, one launch (start us, length us, event | category | flops | bytes accessed | tf_op | source)
XLA Modules:
  0.0 85.7 jit_solution(9900573367276436608)
XLA Ops:
  0.0 84.1 %shard_map.91 = bf16[128,896]{1,0:T(8,128)(2,1)} custom-call(bf16[128,896]{1,0:T(8,128)(2,1)} %refs_0_.1, s32[4,128]{1,0:T(4,128)} %bitcast.8, f32[4,128]{1,0:T(4,128)} %bitcast.9, bf16[3584,512]{1,0:T(8,128)(2,1)} %bitcast.5, bf16[3584,512]{1,0:T(8,128)(2,1)} %bitcast.6, bf16[2048,896]{1,0:T(8,128)(2,1)} %bitcast.7, bf16[3584,512]{1,0:T(8,128)(2,1)} %refs_6_.1, ...), custom_call_target="tpu_custom_call" | custom-call | tf_op jit(solution)/shard_map/pallas_call | solution.py:614
  84.1 1.6 %copy.11 = bf16[128,896]{1,0:T(8,128)(2,1)} copy(bf16[128,896]{1,0:T(8,128)(2,1)} %shard_map.91) | data formatting | bytes 458752

commit v2 on v1

--- a/solution.py
+++ b/solution.py
@@ -140,6 +140,14 @@
     acc_g,
     acc_u,
     hold,
+    blend,
+    rows_out,
+    near_wd,
+    near_part,
+    near_got,
+    near_hold,
+    near_sum,
+    end_sum,
     loc_sem,
     z_send,
     z_recv,
@@ -149,6 +157,10 @@
     m_recv,
     p_send,
     p_recv,
+    w_send,
+    w_recv,
+    x_send,
+    x_recv,
 ):
     ctx_count, group_count, member_count, cap = sizes
     c = lax.axis_index("ctx")
@@ -174,7 +186,7 @@
     first.start()
     loads = []
     for index, (src, dst) in enumerate(
-        ((sg_in, sg), (su_in, su), (wg_in, wg), (wu_in, wu), (sd_in, sd), (wd_in, wd))
+        ((sg_in, sg), (su_in, su), (wg_in, wg), (wu_in, wu), (wd_in, wd), (sd_in, sd))
     ):
         loads.append(pltpu.make_async_copy(src, dst, loc_sem.at[2 + index]))
 
@@ -226,10 +238,14 @@
             device_id_type=MESH,
         )
 
-    def line_send(chunk, depth, finish=False):
+    def line_send(chunk, depth, finish=False, only=None):
         for way in (0, 1):
             shard, target = (c - depth, c + 1) if way == 0 else (c + depth, c - 1)
             ready = (c >= depth) & (c < last) if way == 0 else (c + depth <= last) & (c > 0)
+            if PAIR <= chunk < PAIR + 3 and depth == 0:
+                ready = ready & (c != (last - 1 if way == 0 else 1))
+            if only is not None:
+                ready = ready & only
 
             @pl.when(ready)
             def _():
@@ -251,6 +267,8 @@
                     continue
             else:
                 here = here & (passes if relays else jnp.logical_not(passes))
+            if PAIR <= chunk < PAIR + 3 and depth == 0 and not relays:
+                continue
 
             @pl.when(here)
             def _():
@@ -260,12 +278,22 @@
                 if then is not None:
                     then(shard)
 
-    def relay_line(chunk, depth, then=None):
-        line_take(chunk, depth, True, then)
-
-    def await_line(chunk):
-        for depth in range(last):
+    def await_line(chunk, depths):
+        for depth in depths:
             line_take(chunk, depth, False)
+
+    def relay(chunk, kind):
+        depth = 1 if kind == "far" else 0
+        for way in (0, 1):
+            me = 1 if (way == 0) == (kind == "edge") else last - 1
+            shard = c - 1 - depth if way == 0 else c + 1 + depth
+            source = c - 1 if way == 0 else c + 1
+            target = c + 1 if way == 0 else c - 1
+
+            @pl.when(c == me)
+            def _():
+                line(chunk, depth, way, shard, source).wait_recv()
+                line(chunk, depth + 1, way, shard, target).start()
 
     def at_stage(stage, then):
         if stage == 0:
@@ -297,6 +325,26 @@
 
     line_send(0, 0)
     line_send(1, 0)
+
+    ends = ((0, 1), (last, last - 1))
+    lent = ((0, 3 * width // 4), (3 * width // 4, width // 4))
+
+    def lend(part_index, end, near):
+        return pltpu.make_async_remote_copy(
+            src_ref=wd.at[pl.ds(near * width + lent[part_index][0], lent[part_index][1])],
+            dst_ref=near_wd.at[pl.ds(*lent[part_index])],
+            send_sem=w_send.at[part_index],
+            recv_sem=w_recv.at[part_index],
+            device_id={"ctx": near},
+            device_id_type=MESH,
+        )
+
+    def lend_start(part_index):
+        for end, near in ends:
+
+            @pl.when(c == end)
+            def _():
+                lend(part_index, end, near).start()
 
     scores = scores_in[...]
     scaled = route_scale * scores / jnp.sum(scores, axis=0, keepdims=True)
@@ -350,46 +398,27 @@
         spots = lax.broadcasted_iota(jnp.int32, (cap, tok_count), 0).astype(jnp.float32)
         return jnp.where(spots == rank_of(slot), 1.0, 0.0).astype(jnp.bfloat16)
 
-    def pair_add(shard, fresh=False):
+    def pair_add(index, shard, fresh=False):
         ins = columns(shard)
-        for place, slot in enumerate(pairs[3]):
+        for place, slot in enumerate(pairs[index]):
             chosen = matmul(mask_of(slot), tok[slot, shard]).astype(jnp.bfloat16)
-            rows_in[place * cap : (place + 1) * cap, ins] = chosen
+            rows_in[place * cap : (place + 1) * cap, :] = chosen
 
         def visit(start, size):
             cols = pl.ds(start, size)
-            g = matmul(rows_in[0 : 2 * cap, ins], wg[ins, cols])
-            u = matmul(rows_in[0 : 2 * cap, ins], wu[ins, cols])
-            acc_g[:, cols] = g if fresh else acc_g[:, cols] + g
-            acc_u[:, cols] = u if fresh else acc_u[:, cols] + u
+            g = matmul(rows_in[...], wg[ins, cols])
+            u = matmul(rows_in[...], wu[ins, cols])
+            acc_g[index, :, cols] = g if fresh else acc_g[index, :, cols] + g
+            acc_u[index, :, cols] = u if fresh else acc_u[index, :, cols] + u
 
         column_tiles(width, 256, visit)
 
-    def pick(row, slot):
-        mask = mask_of(slot)
-
-        def step(shard, carry):
-            chosen = matmul(mask, tok[slot, shard]).astype(jnp.bfloat16)
-            rows_in[row : row + cap, columns(shard)] = chosen
-            return carry
-
-        lax.fori_loop(0, ctx_count, step, 0)
-
-    def hidden(count, gate, up, target):
-        def visit(start, size):
-            cols = pl.ds(start, size)
-            g = matmul(rows_in[0:count, :], gate[:, cols])
-            u = matmul(rows_in[0:count, :], up[:, cols])
-            target[:, cols] = (g / (1.0 + jnp.exp(-g)) * u).astype(jnp.bfloat16)
-
-        column_tiles(width, 256, visit)
+    def pair_end(index):
+        g = acc_g[index]
+        hid[index, c] = (g / (1.0 + jnp.exp(-g)) * acc_u[index]).astype(jnp.bfloat16)
+        line_send(PAIR + index, 0)
 
     pairs = ((2, 3), (4, 5), (6, 7), (0, 1))
-
-    def compute(index):
-        for place, slot in enumerate(pairs[index]):
-            pick(place * cap, slot)
-        hidden(2 * cap, wg, wu, hid.at[index, c])
 
     half = ctx_count // 2
 
@@ -400,12 +429,14 @@
     loads[2].wait()
     loads[3].wait()
     take(1, c)
-    pair_add(c, True)
+    pair_add(3, c, True)
+    loads[4].wait()
+    lend_start(0)
 
     def both_add(shard):
         shared_add(shard)
         take(1, shard)
-        pair_add(shard)
+        pair_add(3, shard)
 
     for depth in range(last):
         for chunk, then in ((0, None), (1, spread)):
@@ -413,14 +444,13 @@
                 line_take(chunk, depth, relays, then)
         at_stage(depth + 1, both_add)
 
-    g = acc_g[...]
-    hid[3, c] = (g / (1.0 + jnp.exp(-g)) * acc_u[...]).astype(jnp.bfloat16)
-    line_send(PAIR + 3, 0)
+    pair_end(3)
     g = sum_g[...]
     hid_s[c] = (g / (1.0 + jnp.exp(-g)) * sum_u[...]).astype(jnp.bfloat16)
-    line_send(SHARED, 0)
-
-    def relay(shard):
+    line_send(SHARED, 0, only=inner)
+    lend_start(1)
+
+    def pass_on(shard):
         take(2, shard)
         hand(2, 3, shard, 1).start()
 
@@ -435,42 +465,42 @@
         def _():
             hand(4, 6, shard, 2).start()
 
-    at_stage(0, relay)
-    at_stage(1, relay)
-    relay_line(PAIR + 3, 0)
-    for stage in range(2, ctx_count):
-        at_stage(stage, relay)
+    def absorb(index, stage):
+        def add(shard):
+            take(pairs[index][1], shard)
+            pair_add(index, shard, stage == 0)
+
+        at_stage(stage, add)
+
+    at_stage(0, pass_on)
+    at_stage(1, pass_on)
     for copy in greet[1:]:
         copy.wait_recv()
-    for shard in range(ctx_count):
-        take(3, shard)
-    compute(0)
-    line_send(PAIR, 0)
-    for shard in range(ctx_count):
-        take(5, shard)
-    compute(1)
-    line_send(PAIR + 1, 0)
-    relay_line(PAIR + 3, 1)
-    for shard in range(ctx_count):
-        take(6, shard)
-        hand(6, 7, shard, 1).start()
-    relay_line(PAIR, 0)
-    relay_line(PAIR + 1, 0)
-    for shard in range(ctx_count):
-        take(7, shard)
-    compute(2)
-    line_send(PAIR + 2, 0)
-    relay_line(PAIR, 1)
-
-    loads[4].wait()
+    absorb(0, 0)
+    absorb(1, 0)
+    relay(PAIR + 3, "near")
+    at_stage(2, pass_on)
+    at_stage(3, pass_on)
+    for stage in range(1, ctx_count):
+        absorb(0, stage)
+    relay(PAIR + 3, "edge")
+    pair_end(0)
+    relay(SHARED, "near")
+    for stage in range(1, ctx_count):
+        absorb(1, stage)
+    pair_end(1)
+
     loads[5].wait()
 
-    def product(index, down, cols):
-        value = matmul(hid[index, 0], down[0:width, cols])
-        for shard in range(1, ctx_count):
-            value = value + matmul(
-                hid[index, shard], down[shard * width : (shard + 1) * width, cols]
-            )
+    def product(index, shards, cols):
+        value = None
+        for shard in shards:
+            units = shard * width
+            if not isinstance(shard, int):
+                units = pl.multiple_of(units, 128)
+            units = pl.ds(units, width)
+            term = matmul(hid[index, shard], wd[units, cols])
+            value = term if value is None else value + term
         return value
 
     def shared_out(shard, fresh=False):
@@ -485,11 +515,10 @@
 
     split = -(-out_width // 256) * 128
     parts = ((0, split), (split, out_width - split))
-    sends = {}
 
     def ship(slot, over, part_index):
         cols = pl.ds(*parts[part_index])
-        copy = pltpu.make_async_remote_copy(
+        return pltpu.make_async_remote_copy(
             src_ref=part.at[slot - 1, :, cols],
             dst_ref=got.at[slot - 1, :, cols],
             send_sem=p_send.at[slot, part_index],
@@ -497,64 +526,194 @@
             device_id=peer(over),
             device_id_type=MESH,
         )
-        sends[slot, part_index] = copy
-        copy.start()
 
     def tiles(part_index, visit):
         begin, size = parts[part_index]
-        column_tiles(size, 256, lambda start, count: visit(begin + start, count))
+
+        def shifted(start, count):
+            at = begin + start
+            visit(at if isinstance(at, int) else pl.multiple_of(at, 128), count)
+
+        column_tiles(size, 256, shifted)
+
+    def mix(index, rows, cols, whole, held, outgoing):
+        for place, slot in enumerate(pairs[index]):
+            value = matmul(blend[slot, :, 0:cap], rows[place * cap : (place + 1) * cap])
+            if slot == 0:
+                whole(cols, value)
+            elif place == 0:
+                held[:, cols] = value
+            else:
+                outgoing[slot - 1, :, cols] = value.astype(jnp.bfloat16)
 
     def finish(index):
-        weights = []
-        for slot in pairs[index]:
-            spots = lax.broadcasted_iota(jnp.int32, (tok_count, tok_count), 0).astype(jnp.float32)
-            mask = jnp.where(spots == rank_of(slot), weight_of(slot), 0.0)
-            weights.append(jnp.transpose(mask)[:, 0:cap].astype(jnp.bfloat16))
-
-        def visit(start, size):
-            cols = pl.ds(start if isinstance(start, int) else pl.multiple_of(start, 128), size)
-            rows = product(index, wd, cols).astype(jnp.bfloat16)
-            for place, slot in enumerate(pairs[index]):
-                value = matmul(weights[place], rows[place * cap : (place + 1) * cap])
-                if slot == 0:
-                    total[:, cols] += value
-                elif place == 0:
-                    hold[:, cols] = value
+        def add_total(cols, value):
+            total[:, cols] += value
+
+        for part_index in range(2):
+            if index < 3:
+                for shards, where in (
+                    ((0, 1, 2, 3), inner),
+                    ((c, c + 2, c + 3), c == 0),
+                    ((c, c - 2, c - 3), c == last),
+                ):
+
+                    @pl.when(where)
+                    def _():
+                        def visit(start, size):
+                            cols = pl.ds(start, size)
+                            rows_out[:, cols] = product(index, shards, cols).astype(jnp.bfloat16)
+
+                        tiles(part_index, visit)
+
+            def visit(start, size):
+                cols = pl.ds(start, size)
+                if index < 3:
+                    rows = rows_out[:, cols]
                 else:
-                    part[slot - 1, :, cols] = value.astype(jnp.bfloat16)
-
-        for part_index in range(2):
+                    rows = product(index, range(ctx_count), cols).astype(jnp.bfloat16)
+                mix(index, rows, cols, add_total, hold, part)
+
             tiles(part_index, visit)
-            ship(pairs[index][1], 1, part_index)
+            ship(pairs[index][1], 1, part_index).start()
 
     def forward(index):
         slot, other = pairs[index]
 
         def visit(start, size):
-            cols = pl.ds(start if isinstance(start, int) else pl.multiple_of(start, 128), size)
+            cols = pl.ds(start, size)
             value = hold[:, cols] + got[other - 1, :, cols].astype(jnp.float32)
             part[slot - 1, :, cols] = value.astype(jnp.bfloat16)
 
         for part_index in range(2):
-            sends[other, part_index].wait_recv()
+            ship(other, 1, part_index).wait_recv()
             tiles(part_index, visit)
-            ship(slot, slot, part_index)
-
+            ship(slot, slot, part_index).start()
+
+    def near_ship(slot, over):
+        return pltpu.make_async_remote_copy(
+            src_ref=near_part.at[slot - 1],
+            dst_ref=near_got.at[slot - 1],
+            send_sem=x_send.at[slot],
+            recv_sem=x_recv.at[slot],
+            device_id=peer(over),
+            device_id_type=MESH,
+        )
+
+    def near_finish(index):
+        def visit(start, size):
+            cols = pl.ds(start, size)
+            rows = matmul(hid[index, c], near_wd[:, cols]).astype(jnp.bfloat16)
+            mix(index, rows, cols, None, near_hold.at[index], near_part)
+
+        column_tiles(out_width, 256, visit)
+        near_ship(pairs[index][1], 1).start()
+
+    def near_forward(index):
+        slot, other = pairs[index]
+        near_ship(other, 1).wait_recv()
+
+        def visit(start, size):
+            cols = pl.ds(start, size)
+            value = near_hold[index, :, cols] + near_got[other - 1, :, cols].astype(jnp.float32)
+            near_part[slot - 1, :, cols] = value.astype(jnp.bfloat16)
+
+        column_tiles(out_width, 256, visit)
+        near_ship(slot, slot).start()
+
+    def to_end(end):
+        return pltpu.make_async_remote_copy(
+            src_ref=near_sum,
+            dst_ref=end_sum,
+            send_sem=x_send.at[0],
+            recv_sem=x_recv.at[0],
+            device_id={"ctx": end},
+            device_id_type=MESH,
+        )
+
+    def on_inner(step, *args):
+        @pl.when(inner)
+        def _():
+            step(*args)
+
+    def lent_wait():
+        for part_index in range(2):
+            lend(part_index, c, c).wait_recv()
+
+    def take_pair(shards):
+        for shard in shards:
+            take(6, shard)
+            hand(6, 7, shard, 1).start()
+
+    def add_pair(shards):
+        for shard in shards:
+            take(7, shard)
+            pair_add(2, shard, shard == 0)
+
+    for slot in range(tok.shape[0]):
+        spots = lax.broadcasted_iota(jnp.int32, (tok_count, tok_count), 0).astype(jnp.float32)
+        mask = jnp.where(spots == rank_of(slot), weight_of(slot), 0.0)
+        blend[slot] = jnp.transpose(mask).astype(jnp.bfloat16)
+    relay(PAIR + 3, "far")
+    take_pair(range(half))
+    add_pair(range(half))
+    relay(PAIR, "near")
+    relay(PAIR, "edge")
+    take_pair(range(half, ctx_count))
+    add_pair(range(half, ctx_count - 1))
+    relay(PAIR + 1, "near")
+    relay(PAIR + 1, "edge")
+    add_pair(range(ctx_count - 1, ctx_count))
+    pair_end(2)
+    line_send(SHARED, 0, only=jnp.logical_not(inner))
+    on_inner(lent_wait)
+    on_inner(near_finish, 0)
+    relay(PAIR, "far")
+    on_inner(near_finish, 2)
+    relay(PAIR + 2, "edge")
+    relay(PAIR + 1, "far")
+    on_inner(near_finish, 1)
+    on_inner(near_forward, 2)
+    on_inner(near_forward, 0)
+    on_inner(near_forward, 1)
+    relay(PAIR + 2, "near")
+    relay(SHARED, "edge")
+    relay(PAIR + 2, "far")
     shared_out(c, True)
-    await_line(PAIR + 3)
+    await_line(PAIR + 3, range(last))
     finish(3)
-    relay_line(PAIR + 1, 1)
-    relay_line(PAIR + 2, 0)
-    relay_line(PAIR + 2, 1)
-    relay_line(SHARED, 0)
-    relay_line(SHARED, 1)
-    await_line(PAIR)
+    relay(SHARED, "far")
+    await_line(PAIR, range(last))
     finish(0)
     forward(0)
-    await_line(PAIR + 1)
+
+    @pl.when(inner)
+    def _():
+        for slot in (2, 4, 6):
+            near_ship(slot, slot).wait_recv()
+
+        def visit(start, size):
+            cols = pl.ds(start, size)
+            value = near_got[1, :, cols].astype(jnp.float32)
+            for slot in (4, 6):
+                value = value + near_got[slot - 1, :, cols].astype(jnp.float32)
+            near_sum[:, cols] = value.astype(jnp.bfloat16)
+
+        column_tiles(out_width, 256, visit)
+
+    for end, near in ends:
+
+        @pl.when(c == near)
+        def _():
+            to_end(end).start()
+
+    await_line(PAIR + 1, range(last))
     finish(1)
     forward(1)
-    await_line(PAIR + 2)
+    await_line(SHARED, range(last - 1))
+    for stage in range(1, last):
+        at_stage(stage, shared_out)
+    await_line(PAIR + 2, range(last))
     finish(2)
     forward(2)
 
@@ -567,23 +726,47 @@
 
     for slot in (1, 2, 4):
         for part_index in range(2):
-            sends[slot, part_index].wait_recv()
+            ship(slot, slot, part_index).wait_recv()
     column_tiles(out_width, 256, gather_some)
-    await_line(SHARED)
-    for depth in range(last):
-        at_stage(depth + 1, shared_out)
+    await_line(SHARED, (last - 1,))
+    at_stage(last, shared_out)
+
+    @pl.when(jnp.logical_not(inner))
+    def _():
+        to_end(c).wait_recv()
+
+        def visit(start, size):
+            cols = pl.ds(start, size)
+            total[:, cols] += end_sum[:, cols].astype(jnp.float32)
+
+        column_tiles(out_width, 256, visit)
 
     def gather_rest(start, size):
-        cols = pl.ds(start if isinstance(start, int) else pl.multiple_of(start, 128), size)
+        cols = pl.ds(start, size)
         value = total[:, cols] + got[5, :, cols].astype(jnp.float32)
         out_ref[:, cols] = value.astype(jnp.bfloat16)
 
     for part_index in range(2):
-        sends[6, part_index].wait_recv()
+        ship(6, 6, part_index).wait_recv()
         tiles(part_index, gather_rest)
 
-    for copy in list(sends.values()) + greet:
+    for slot in slots:
+        for part_index in range(2):
+            ship(slot, slot, part_index).wait_send()
+    for copy in greet:
         copy.wait_send()
+
+    @pl.when(inner)
+    def _():
+        for slot in slots[1:]:
+            near_ship(slot, slot).wait_send()
+        to_end(c).wait_send()
+
+    @pl.when(jnp.logical_not(inner))
+    def _():
+        for part_index in range(2):
+            lend(part_index, c, 1).wait_send()
+
     for chunk in range(PAIR + 4):
         for depth in range(last):
             line_send(chunk, depth, finish=True)
@@ -606,7 +789,6 @@
     meta_rows = -(-(group_count + expert_count) // 16) * 16
     slots = 2 * group_count
     bf16 = jnp.bfloat16
-    rows = max(2 * cap, tok_count)
     anywhere = pl.BlockSpec(memory_space=pl.ANY)
     inside = pl.BlockSpec(memory_space=pltpu.VMEM)
     dma = pltpu.SemaphoreType.DMA
@@ -625,7 +807,7 @@
             pltpu.VMEM(shared_gate.shape, bf16),
             pltpu.VMEM(shared_up.shape, bf16),
             pltpu.VMEM(shared_down.shape, bf16),
-            pltpu.VMEM((rows, ctx_count * feat), bf16),
+            pltpu.VMEM((2 * cap, feat), bf16),
             pltpu.VMEM((ctx_count, tok_count, width), bf16),
             pltpu.VMEM((4, ctx_count, 2 * cap, width), bf16),
             pltpu.VMEM((slots - 1, tok_count, out_width), bf16),
@@ -633,9 +815,17 @@
             pltpu.VMEM((tok_count, out_width), jnp.float32),
             pltpu.VMEM((tok_count, width), jnp.float32),
             pltpu.VMEM((tok_count, width), jnp.float32),
-            pltpu.VMEM((2 * cap, width), jnp.float32),
-            pltpu.VMEM((2 * cap, width), jnp.float32),
+            pltpu.VMEM((4, 2 * cap, width), jnp.float32),
+            pltpu.VMEM((4, 2 * cap, width), jnp.float32),
             pltpu.VMEM((tok_count, out_width), jnp.float32),
+            pltpu.VMEM((slots, tok_count, tok_count), bf16),
+            pltpu.VMEM((2 * cap, out_width), bf16),
+            pltpu.VMEM((width, out_width), bf16),
+            pltpu.VMEM((slots - 1, tok_count, out_width), bf16),
+            pltpu.VMEM((slots - 1, tok_count, out_width), bf16),
+            pltpu.VMEM((3, tok_count, out_width), jnp.float32),
+            pltpu.VMEM((tok_count, out_width), bf16),
+            pltpu.VMEM((tok_count, out_width), bf16),
             dma((8,)),
             dma((2, ctx_count - 1, 7)),
             dma((2, ctx_count - 1, 7)),
@@ -645,6 +835,10 @@
             dma((slots,)),
             dma((slots, 2)),
             dma((slots, 2)),
+            dma((2,)),
+            dma((2,)),
+            dma((slots,)),
+            dma((slots,)),
         ],
         compiler_params=pltpu.CompilerParams(
             collective_id=0, has_side_effects=True, vmem_limit_bytes=VMEM_BYTES
@@ -664,7 +858,8 @@
 
 def local(tokens, expert_ids, *rest):
     whole_groups = expert_ids.shape[1] == 2 * lax.axis_size("local")
-    if whole_groups and lax.axis_size("local") == 2 and lax.axis_size("node") == 4:
+    sizes = (lax.axis_size("ctx"), lax.axis_size("node"), lax.axis_size("local"))
+    if whole_groups and sizes == (4, 4, 2):
         return cube(tokens, expert_ids, *rest)
     return exchange(tokens, expert_ids, *rest)
 

time: 85.9 us -> 82.9 us (0.965)
  the two profiles are of different devices: /device:TPU:0 before, /device:TPU:13 now
where the time goes in v2:
time: 82.9 us; the launch traced here: 82.8 us
  Pallas kernels  81.1 us (98%)
  local copies, waits for them, and re-layouts  1.65 us (2%)
    pallas_call x1, Pallas kernels, cube(): pl.pallas_call(kernel, out_shape=jax.ShapeDtypeStruct((tok_count, out_wid...  81.1 us

profile of v2, /device:TPU:13, one launch (start us, length us, event | category | flops | bytes accessed | tf_op | source)
XLA Modules:
  0.0 82.8 jit_solution(10482387706241587328)
XLA Ops:
  0.0 81.1 %shard_map.91 = bf16[128,896]{1,0:T(8,128)(2,1)} custom-call(bf16[128,896]{1,0:T(8,128)(2,1)} %refs_0_.1, s32[4,128]{1,0:T(4,128)} %bitcast.8, f32[4,128]{1,0:T(4,128)} %bitcast.9, bf16[3584,512]{1,0:T(8,128)(2,1)} %bitcast.5, bf16[3584,512]{1,0:T(8,128)(2,1)} %bitcast.6, bf16[2048,896]{1,0:T(8,128)(2,1)} %bitcast.7, bf16[3584,512]{1,0:T(8,128)(2,1)} %refs_6_.1, ...), custom_call_target="tpu_custom_call" | custom-call | tf_op jit(solution)/shard_map/pallas_call | solution.py:796
  81.1 1.6 %copy.11 = bf16[128,896]{1,0:T(8,128)(2,1)} copy(bf16[128,896]{1,0:T(8,128)(2,1)} %shard_map.91) | data formatting | bytes 458752

commit v3 on v2

--- a/solution.py
+++ b/solution.py
@@ -679,13 +679,26 @@
     relay(PAIR + 2, "near")
     relay(SHARED, "edge")
     relay(PAIR + 2, "far")
-    shared_out(c, True)
     await_line(PAIR + 3, range(last))
-    finish(3)
-    relay(SHARED, "far")
+
+    def own_part():
+        shared_out(c, True)
+        finish(3)
+
+    def shared_part():
+        for stage in range(1, last):
+            at_stage(stage, shared_out)
+
+    outer = jnp.logical_not(inner)
+
+    @pl.when(outer)
+    def _():
+        own_part()
+
     await_line(PAIR, range(last))
     finish(0)
     forward(0)
+    relay(SHARED, "far")
 
     @pl.when(inner)
     def _():
@@ -711,11 +724,19 @@
     finish(1)
     forward(1)
     await_line(SHARED, range(last - 1))
-    for stage in range(1, last):
-        at_stage(stage, shared_out)
+
+    @pl.when(outer)
+    def _():
+        shared_part()
+
     await_line(PAIR + 2, range(last))
     finish(2)
     forward(2)
+
+    @pl.when(inner)
+    def _():
+        own_part()
+        shared_part()
 
     def gather_some(start, size):
         cols = pl.ds(start, size)

time: 82.9 us -> 82.4 us (level)
  the two profiles are of different devices: /device:TPU:13 before, /device:TPU:15 now
where the time goes in v3:
time: 82.4 us; the launch traced here: 82.3 us
  Pallas kernels  80.6 us (98%)
  local copies, waits for them, and re-layouts  1.65 us (2%)
    pallas_call x1, Pallas kernels, cube(): pl.pallas_call(kernel, out_shape=jax.ShapeDtypeStruct((tok_count, out_wid...  80.6 us

profile of v3, /device:TPU:15, one launch (start us, length us, event | category | flops | bytes accessed | tf_op | source)
XLA Modules:
  0.0 82.3 jit_solution(716289778808857374)
XLA Ops:
  0.0 80.6 %shard_map.91 = bf16[128,896]{1,0:T(8,128)(2,1)} custom-call(bf16[128,896]{1,0:T(8,128)(2,1)} %refs_0_.1, s32[4,128]{1,0:T(4,128)} %bitcast.8, f32[4,128]{1,0:T(4,128)} %bitcast.9, bf16[3584,512]{1,0:T(8,128)(2,1)} %bitcast.5, bf16[3584,512]{1,0:T(8,128)(2,1)} %bitcast.6, bf16[2048,896]{1,0:T(8,128)(2,1)} %bitcast.7, bf16[3584,512]{1,0:T(8,128)(2,1)} %refs_6_.1, ...), custom_call_target="tpu_custom_call" | custom-call | tf_op jit(solution)/shard_map/pallas_call | solution.py:817
  80.6 1.6 %copy.11 = bf16[128,896]{1,0:T(8,128)(2,1)} copy(bf16[128,896]{1,0:T(8,128)(2,1)} %shard_map.91) | data formatting | bytes 458752
